TPU v7x, 32 devices: a whole 2x2x4 slice. The times are simulated.
32 devices in a mesh: dp: 4 (over y, x), region: 8 (over z, core).
Axes of the slice: x: 2, y: 2, z: 4, core: 2. Of those that a mesh axis runs over, the one named last changes fastest.
Arguments:
- features: bfloat16 [4, 8, 16, 16, 16, 128], P('dp', 'region'), may hold values from -6 to 6
- conv_weight: bfloat16 [3, 3, 3, 128, 128], replicated, may hold values from -0.109375 to 0.109375
- down_weight: bfloat16 [2, 2, 2, 128, 128], replicated, may hold values from -0.1875 to 0.1875
- coarse_cotangent: bfloat16 [4, 8, 16, 16, 16, 128], P('dp', 'region'), may hold values from -6 to 6
- brick_coords: int32 [4, 8, 3], P('dp', 'region'), may hold values from 0 to 7, as said below
- neighbours: int32 [4, 8, 26], P('dp', 'region'), may hold values from -1 to 7, as said below
- parents: int32 [4, 8], P('dp', 'region'), may hold values from 0 to 7, as said below
Outputs:
- coarse_features: bfloat16 [4, 8, 16, 16, 16, 128], P('dp', 'region')
- input_grad: bfloat16 [4, 8, 16, 16, 16, 128], P('dp', 'region')
- conv_grad: float32 [3, 3, 3, 128, 128], replicated
- down_grad: float32 [2, 2, 2, 128, 128], replicated
Inputs may be any that keep to these rules, and one draw needn't show every extreme that they name: `brick_coords`: slot s lies on region index s; its first coordinate is s, the second below 4, the third below 2; the coordinates of one scene's slots are distinct. `neighbours`: entry d names the slot whose coordinates are the brick's own plus offset d, or -1 where no slot has them; named slots lie on the same or an adjacent region index, and the relation is symmetric. `parents`: the parent is 2 (x // 2) + (y // 2) of the brick's coordinates; coarse brick c lies on region index c.
All inputs are finite; a program needn't handle non-finite values.
Results may differ from a plain program's by a relative error of at most 0.005.
Values may be sent and summed in bfloat16 or wider, within the bound.
A program may use at most 192 MiB of HBM per device.

v0:
```python
import functools

import jax
import jax.numpy as jnp
from jax import lax
from jax.experimental import pallas as pl
from jax.experimental.pallas import tpu as pltpu
from jax.sharding import PartitionSpec as P

loss_scale = 1024.0
MESH = pl.DeviceIdType.MESH
F32, BF16 = jnp.float32, jnp.bfloat16


def passed_along(value, axis, by):
    peers = lax.axis_size(axis)
    pairs = [(i, i + by) for i in range(peers) if 0 <= i + by < peers]
    return lax.ppermute(value, axis, pairs)


def partner(block, axis):
    count = lax.axis_size(axis)
    return lax.ppermute(block, axis, [(i, i ^ 1) for i in range(count)])


def nn(a, b):
    return lax.dot_general(a, b, (((1,), (0,)), ((), ())), preferred_element_type=F32)


def nt(a, b):
    return lax.dot_general(a, b, (((1,), (1,)), ((), ())), preferred_element_type=F32)


def shifted(s, low, mid, high):
    edge = s.shape[-2]
    axis = s.ndim - 2
    row = lax.broadcasted_iota(jnp.int32, s.shape, axis)
    first = pltpu.roll(s, 1, axis) * jnp.where(row == 0, low, mid)
    last = pltpu.roll(s, edge - 1, axis) * jnp.where(row == edge - 1, high, mid)
    return first, s * mid, last


def put_plane(dst, x, even, odd, low, mid, high):
    half, c = even.shape[0], even.shape[-1]
    for k, v in enumerate(shifted(even, low, mid, high)):
        dst[x, 0:half, :, 2 * k * c + c : 2 * k * c + 2 * c] = v.astype(BF16)
    for k, v in enumerate(shifted(odd, low, mid, high)):
        dst[x, 1 : half + 1, :, 2 * k * c : 2 * k * c + c] = v.astype(BF16)


def put_row(dst, x, y, row, low, mid, high):
    c = row.shape[-1]
    for k, v in enumerate(shifted(row, low, mid, high)):
        at = 2 * k * c + (y % 2) * c
        dst[x, y // 2, :, at : at + c] = v.astype(BF16)


def masks(nb, a):
    def m(b, c):
        i = (a + 1) * 9 + (b + 1) * 3 + (c + 1)
        i = i - 1 if i > 13 else i
        return jnp.where(nb[i] >= 0, 1.0, 0.0).astype(F32)

    return {b: (m(b, -1), m(b, 0), m(b, 1)) for b in (-1, 0, 1)}


def put_halo(dst, x, even, odd, mask):
    half, edge = even.shape[0], dst.shape[0]
    put_plane(dst, x, even, odd, *mask[0])
    put_row(dst, x, 0, odd[half - 1], *mask[-1])
    put_row(dst, x, edge - 1, even[0], *mask[1])


def zero_rows(dst, edge, c):
    z = jnp.zeros((edge, dst.shape[2], c), BF16)
    for k in range(3):
        dst[1 : edge + 1, 0, :, 2 * k * c : 2 * k * c + c] = z
        dst[1 : edge + 1, edge // 2, :, 2 * k * c + c : 2 * k * c + 2 * c] = z


def tap_of(s, pin, pout):
    b = 2 * s + pin - pout
    return b if 0 <= b <= 2 else None


def compute_kernel(
    nb, f, flo, fhi, ch, clo, chi, cw, dw, blocks, ig, acc,
    field, wide, gfold, up, outf, gt, tt,
):
    edge, c = f.shape[0], f.shape[-1]
    half = edge // 2
    rows = half * edge

    def window(x, n, a, s):
        return field[pl.ds(x + a, n), s : s + half].reshape(n * rows, 6 * c)

    def lhs(x, n):
        return jnp.concatenate([window(x, n, a, s) for a in range(3) for s in range(2)], -1)

    def lift(v, shape):
        up[...] = jnp.zeros_like(up)
        n = v.shape[0] * v.shape[1]
        v = v.astype(F32).reshape(n, half, c)
        for r in range(2):
            up[r, 0:n, pl.ds(r, half, 2), :] = v
        both = [up[r, 0:n].reshape(n * edge, c).astype(BF16) for r in range(2)]
        return jnp.concatenate(both, -1)

    def dwt(p):
        return jnp.concatenate(
            [jnp.concatenate([dw[4 * p + 2 * q + r] for r in range(2)], -1) for q in range(2)], 0
        )

    raised = lift(ch[...], None)
    for p in range(2):
        g = nt(raised, dwt(p)).astype(BF16).reshape(half, half, edge, 2 * c)
        for i in range(half):
            gfold[2 * i + p] = g[i]
    glo = nt(lift(clo[...][None], None), dwt(1)).astype(BF16).astype(F32)
    ghi = nt(lift(chi[...][None], None), dwt(0)).astype(BF16).astype(F32)
    glo = glo.reshape(half, edge, 2 * c)
    ghi = ghi.reshape(half, edge, 2 * c)

    below, above = masks(nb, -1), masks(nb, 1)
    zero_rows(field, edge, c)
    put_halo(field, 0, flo[:, 0].astype(F32), flo[:, 1].astype(F32), below)
    put_halo(field, edge + 1, fhi[:, 0].astype(F32), fhi[:, 1].astype(F32), above)

    @pl.loop(0, edge)
    def _(x):
        put_plane(field, x + 1, f[x, :, 0].astype(F32), f[x, :, 1].astype(F32), 0.0, 1.0, 0.0)

    flat = gfold[...].reshape(edge * rows, 2 * c)
    gt[...] = flat.astype(F32).T.astype(BF16)
    for a in range(3):
        for s in range(2):
            tt[s] = nn(gt[...], window(0, edge, a, s))
        for b in range(3):
            for k in range(3):
                total = jnp.zeros((c, c), F32)
                for s in range(2):
                    for pin in range(2):
                        for pout in range(2):
                            if tap_of(s, pin, pout) == b:
                                at = (2 * k + pin) * c
                                total += tt[s, pout * c : (pout + 1) * c, at : at + c]
                tap = 9 * a + 3 * b + k
                acc[tap * c : (tap + 1) * c] = total.T * (1.0 / loss_scale)

    zero = jnp.zeros((c, c), BF16)
    for a in range(3):
        for s in range(2):
            for k in range(3):
                for pin in range(2):
                    at = ((2 * a + s) * 3 + k) * 2 * c + pin * c
                    for pout in range(2):
                        b = tap_of(s, pin, pout)
                        wide[at : at + c, pout * c : (pout + 1) * c] = (
                            zero if b is None else cw[9 * a + 3 * b + k]
                        )
    step = 4

    @pl.loop(0, edge // step)
    def _(n):
        x = n * step
        out = nn(lhs(x, step), wide[...]).reshape(step, half, edge, 2 * c)
        for q in range(2):
            own = f[pl.ds(x, step), :, q].astype(F32)
            outf[q, pl.ds(x, step)] = (
                (out[..., q * c : (q + 1) * c] + own).astype(BF16).astype(F32)
            )

    taken = []
    for p in range(2):
        for r in range(2):
            halves = []
            for q in range(2):
                parts = [
                    outf[q, 2 * i + p, :, pl.ds(r, half, 2), :].reshape(half * half, c)
                    for i in range(half)
                ]
                halves.append(jnp.concatenate(parts, 0).astype(BF16))
            taken.append(jnp.concatenate(halves, -1))
    dwf = jnp.concatenate(
        [dw[4 * p + 2 * q + r] for p in range(2) for r in range(2) for q in range(2)], 0
    )
    blocks[...] = nn(jnp.concatenate(taken, -1), dwf).astype(BF16).reshape(blocks.shape)
    cht = ch[...].reshape(half**3, c).astype(F32).T.astype(BF16)
    for p in range(2):
        for r in range(2):
            d = nn(cht, taken[2 * p + r])
            for q in range(2):
                at = (27 + 4 * p + 2 * q + r) * c
                acc[at : at + c] = d[:, q * c : (q + 1) * c].T * (1.0 / loss_scale)
    rest = acc.shape[0] - 35 * c
    if rest:
        acc[35 * c :] = jnp.zeros((rest, c), F32)

    put_halo(field, 0, glo[..., :c], glo[..., c:], below)
    put_halo(field, edge + 1, ghi[..., :c], ghi[..., c:], above)

    @pl.loop(0, edge)
    def _(x):
        g = gfold[x].astype(F32)
        put_plane(field, x + 1, g[..., :c], g[..., c:], 0.0, 1.0, 0.0)

    for a in range(3):
        for s in range(2):
            for k in range(3):
                for pin in range(2):
                    for pout in range(2):
                        b = tap_of(s, pin, pout)
                        at = ((2 * a + s) * 3 + k) * 2 * c + pin * c
                        wt = zero if b is None else cw[9 * (2 - a) + 3 * (2 - b) + 2 - k]
                        wide[at : at + c, pout * c : (pout + 1) * c] = (
                            zero if b is None else wt.T
                        )

    @pl.loop(0, edge // step)
    def _(n):
        x = n * step
        out = nn(lhs(x, step), wide[...]).reshape(step, half, edge, 2 * c)
        out = (out + gfold[pl.ds(x, step)].astype(F32)).astype(BF16)
        for q in range(2):
            ig[pl.ds(x, step), :, q] = out[..., q * c : (q + 1) * c]


def compute(nb, f, flo, fhi, ch, clo, chi, cw, dw, acc_rows):
    edge, c = f.shape[0], f.shape[-1]
    half = edge // 2
    vmem = pl.BlockSpec(memory_space=pltpu.VMEM)
    return pl.pallas_call(
        compute_kernel,
        out_shape=(
            jax.ShapeDtypeStruct((half, half, half, c), BF16),
            jax.ShapeDtypeStruct((edge, half, 2, edge, c), BF16),
            jax.ShapeDtypeStruct((acc_rows, c), F32),
        ),
        in_specs=[pl.BlockSpec(memory_space=pltpu.SMEM)] + [vmem] * 8,
        out_specs=(vmem, vmem, vmem),
        scratch_shapes=[
            pltpu.VMEM((edge + 2, half + 1, edge, 6 * c), BF16),
            pltpu.VMEM((36 * c, 2 * c), BF16),
            pltpu.VMEM((edge, half, edge, 2 * c), BF16),
            pltpu.VMEM((2, half * half, edge, c), F32),
            pltpu.VMEM((2, edge, half, edge, c), F32),
            pltpu.VMEM((2 * c, edge * half * edge), BF16),
            pltpu.VMEM((2, 2 * c, 6 * c), F32),
        ],
        compiler_params=pltpu.CompilerParams(vmem_limit_bytes=60 * 1024 * 1024),
    )(nb, f.reshape(edge, half, 2, edge, c), flo.reshape(half, 2, edge, c),
      fhi.reshape(half, 2, edge, c), ch, clo, chi, cw, dw)


def reduce_kernel(
    dps, zs, acc, conv, down, from_core, half_sum, to_dp, from_dp, quarter, to_z, from_z, whole,
    s1, r1, s2, r2, s3, r3, s4, r4, s5, r5, s6, r6,
):
    dp, region = lax.axis_index("dp"), lax.axis_index("region")
    core, z = lax.rem(region, 2), lax.div(region, 2)
    total = acc.shape[0]
    h = total // 2
    q = h // dps
    s = q // zs
    mate = (dp, region + 1 - 2 * core)

    def dp_at(k):
        return lax.rem(dp + k, dps)

    def z_at(k):
        return lax.rem(z + k, zs)

    peers = [mate]
    peers += [(dp_at(k), region) for k in range(1, dps)]
    peers += [(dp, 2 * z_at(k) + core) for k in range(1, zs)]
    barrier = pltpu.get_barrier_semaphore()
    for peer in peers:
        pl.semaphore_signal(barrier, inc=1, device_id=peer, device_id_type=MESH)
    pl.semaphore_wait(barrier, len(peers))

    def send(src, dst, ss, rs, to):
        copy = pltpu.make_async_remote_copy(
            src_ref=src, dst_ref=dst, send_sem=ss, recv_sem=rs, device_id=to, device_id_type=MESH
        )
        copy.start()
        return copy

    def rows(start, n):
        return pl.ds(pl.multiple_of(start, 16), n)

    copy = send(acc.at[rows((1 - core) * h, h)], from_core, s1.at[0], r1.at[0], mate)
    copy.wait()
    half_sum[...] = acc[rows(core * h, h)] + from_core[...]
    to_dp[...] = half_sum[...].astype(BF16)
    copies = [
        send(to_dp.at[rows(dp_at(k) * q, q)], from_dp.at[k - 1], s2.at[k - 1], r2.at[k - 1],
             (dp_at(k), region))
        for k in range(1, dps)
    ]
    for copy in copies:
        copy.wait()
    part = half_sum[rows(dp * q, q)]
    for k in range(1, dps):
        part += from_dp[k - 1].astype(F32)
    quarter[...] = part
    to_z[...] = part.astype(BF16)
    copies = [
        send(to_z.at[rows(z_at(k) * s, s)], from_z.at[k - 1], s3.at[k - 1], r3.at[k - 1],
             (dp, 2 * z_at(k) + core))
        for k in range(1, zs)
    ]
    for copy in copies:
        copy.wait()
    part = quarter[rows(z * s, s)]
    for k in range(1, zs):
        part += from_z[k - 1].astype(F32)
    mine = core * h + dp * q
    whole[rows(mine + z * s, s)] = part.astype(BF16)

    def spread(start, n, ss, rs, targets):
        at = whole.at[rows(start, n)]
        copies = [send(at, at, ss.at[i], rs.at[i], to) for i, to in enumerate(targets)]
        for copy in copies:
            copy.wait()

    spread(mine + z * s, s, s4, r4, [(dp, 2 * z_at(k) + core) for k in range(1, zs)])
    spread(mine, q, s5, r5, [(dp_at(k), region) for k in range(1, dps)])
    spread(core * h, h, s6, r6, [mate])
    n = conv.shape[0]
    conv[...] = whole[:n].astype(F32)
    down[...] = whole[n : n + down.shape[0]].astype(F32)


def reduce_all(acc, c):
    dps, zs = lax.axis_size("dp"), lax.axis_size("region") // 2
    total = acc.shape[0]
    h = total // 2
    q = h // dps
    s = q // zs
    vmem = pl.BlockSpec(memory_space=pltpu.VMEM)
    sems = []
    for n in (1, dps - 1, zs - 1, zs - 1, dps - 1, 1):
        sems += [pltpu.SemaphoreType.DMA((n,))] * 2
    return pl.pallas_call(
        functools.partial(reduce_kernel, dps, zs),
        out_shape=(
            jax.ShapeDtypeStruct((27 * c, c), F32),
            jax.ShapeDtypeStruct((8 * c, c), F32),
        ),
        in_specs=[vmem],
        out_specs=(vmem, vmem),
        scratch_shapes=[
            pltpu.VMEM((h, c), F32),
            pltpu.VMEM((h, c), F32),
            pltpu.VMEM((h, c), BF16),
            pltpu.VMEM((dps - 1, q, c), BF16),
            pltpu.VMEM((q, c), F32),
            pltpu.VMEM((q, c), BF16),
            pltpu.VMEM((zs - 1, s, c), BF16),
            pltpu.VMEM((total, c), BF16),
        ] + sems,
        compiler_params=pltpu.CompilerParams(
            collective_id=0, has_side_effects=True, vmem_limit_bytes=32 * 1024 * 1024
        ),
    )(acc)


def octants(block, index):
    half = block.shape[0] // 2
    starts = (index // 4 * half, index // 2 % 2 * half, index % 2 * half, 0)
    return lax.dynamic_slice(block, starts, (half, half, half, block.shape[-1]))


def local(features, conv_weight, down_weight, coarse_cotangent, brick_coords, neighbours, parents):
    edge, c = features.shape[2], features.shape[-1]
    half = edge // 2
    region = lax.axis_index("region")
    peers = lax.axis_size("dp") * lax.axis_size("region")
    f = features.reshape(edge, edge, edge, c)
    cot = coarse_cotangent.reshape(edge, edge, edge, c)
    xyz = brick_coords.reshape(3)
    octant = xyz[0] % 2 * 4 + xyz[1] % 2 * 2 + xyz[2] % 2
    at_home = parents.reshape(()) == region

    other_cot = partner(cot, "region")
    flo = passed_along(f[edge - 1], "region", 1)
    fhi = passed_along(f[0], "region", -1)
    chosen = jnp.where(at_home, octants(cot, octant), octants(other_cot, octant))
    clo = passed_along(chosen[half - 1], "region", 1)
    chi = passed_along(chosen[0], "region", -1)

    unit = 16 * peers
    acc_rows = -(-35 * c // unit) * unit
    blocks, ig, acc = compute(
        neighbours.reshape(26), f, flo, fhi, chosen, clo, chi,
        conv_weight.reshape(27, c, c), down_weight.reshape(8, c, c), acc_rows,
    )
    conv_total, down_total = reduce_all(acc, c)

    tag = jnp.stack([parents.reshape(()), octant])
    other_blocks, other_tag = partner((blocks, tag), "region")
    own_at = jnp.where(at_home, octant, -1)
    other_at = jnp.where(other_tag[0] == region, other_tag[1], -1)
    grid = lambda axis: lax.broadcasted_iota(jnp.int32, (2, 1, 2, 1, 2, 1, 1), axis)
    number = grid(0) * 4 + grid(2) * 2 + grid(4)
    spread = lambda b: b.astype(F32).reshape(1, half, 1, half, 1, half, c)
    coarse = jnp.where(number == own_at, spread(blocks), 0.0) + jnp.where(
        number == other_at, spread(other_blocks), 0.0
    )
    return (
        coarse.astype(BF16).reshape(1, 1, edge, edge, edge, c),
        ig.reshape(1, 1, edge, edge, edge, c),
        conv_total.reshape(3, 3, 3, c, c),
        down_total.reshape(2, 2, 2, c, c),
    )


def solution(mesh):
    in_specs = (
        P("dp", "region", None, None, None, None),
        P(),
        P(),
        P("dp", "region", None, None, None, None),
        P("dp", "region", None),
        P("dp", "region", None),
        P("dp", "region"),
    )
    out_specs = (
        P("dp", "region", None, None, None, None),
        P("dp", "region", None, None, None, None),
        P(),
        P(),
    )
    return jax.shard_map(local, mesh=mesh, in_specs=in_specs, out_specs=out_specs, check_vma=False)
```

profile of v0, /device:TPU:0, one launch (start us, length us, event | category | flops | bytes accessed | tf_op | source)
XLA Modules:
  0.0 89.0 jit_solution(41025898077081365)
XLA Ops:
  0.6 0.6 collective-permute-start.2
  1.2 1.4 %fusion.3 = (s32[1,1,1]{2,1,0:T(1,128)}, s32[1,1,1]{2,1,0:T(1,128)}, s32[1,1,1]{2,1,0:T(1,128)}) fusion(s32[1,1,3]{2,1,0:T(1,128)} %param.11), kind=kLoop, calls=%fused_computation.13 | loop fusion | bytes 24 | tf_op jit(solution)/shard_map/slice | solution.py:382
  9.0 0.1 pad_add_fusion
  9.1 0.0 collective-permute-start.5
  9.1 0.9 slice_bitcast_fusion
  10.0 1.3 %collective-permute-start.1 = (bf16[16,16,128]{2,1,0:T(8,128)(2,1)S(1)}, bf16[16,16,128]{2,1,0:T(8,128)(2,1)S(1)}, u32[]{:S(2)}, u32[]{:S(2)}) collective-permute-start(bf16[16,16,128]{2,1,0:T(8,128)(2,1)S(1)} %get-tuple-element.14), channel_id=1, source_target_pairs={{1,0},{2,1},{3,2},{4,3},{5,4},{6,5},{7,6},{9,8},{10,9},{11,10},{12... | collective-permute-start | bytes 196616 | tf_op jit(solution)/shard_map/ppermute | solution.py:18
  11.3 3.0 %collective-permute-start = (bf16[16,16,128]{2,1,0:T(8,128)(2,1)S(1)}, bf16[16,16,128]{2,1,0:T(8,128)(2,1)S(1)}, u32[]{:S(2)}, u32[]{:S(2)}) collective-permute-start(bf16[16,16,128]{2,1,0:T(8,128)(2,1)S(1)} %get-tuple-element.15), channel_id=1, source_target_pairs={{0,1},{1,2},{2,3},{3,4},{4,5},{5,6},{6,7},{8,9},{9,10},{10,11},{11... | collective-permute-start | bytes 196616 | tf_op jit(solution)/shard_map/ppermute | solution.py:18
  14.5 0.0 collective-permute-done.2
  14.5 1.0 %bitcast_select_fusion.ch = bf16[8,8,8,128]{3,2,1,0:T(8,128)(2,1)S(1)} fusion(bf16[16,16,16,128]{3,2,1,0:T(8,128)(2,1)S(1)} %collective-permute-done.2, s32[]{:T(128)S(6)} %select_n.90, s32[]{:T(128)S(6)} %select_n.93, s32[]{:T(128)S(6)} %select_n.95, bf16[1,1,16,16,16,128]{5,4,3,2,1,0:T(8,128)(2,1)} %param.10, pred[]{:T(512)S(6)} %eq.36), kind=kLoop, calls=%fused_computation.1 | loop fusion | flops 65536 | bytes 393229 | tf_op jit(solution)/shard_map/jit(_where)/select_n | solution.py:388
  15.4 0.0 copy-start.1
  15.5 1.3 %collective-permute-start.4 = (bf16[8,8,128]{2,1,0:T(8,128)(2,1)S(1)}, bf16[8,8,128]{2,1,0:T(8,128)(2,1)S(1)}, u32[]{:S(2)}, u32[]{:S(2)}) collective-permute-start(bf16[8,8,128]{2,1,0:T(8,128)(2,1)S(1)} %get-tuple-element.16), channel_id=1, source_target_pairs={{1,0},{2,1},{3,2},{4,3},{5,4},{6,5},{7,6},{9,8},{10,9},{11,10},{12... | collective-permute-start | bytes 49160 | tf_op jit(solution)/shard_map/ppermute | solution.py:18
  16.8 5.2 %collective-permute-start.3 = (bf16[8,8,128]{2,1,0:T(8,128)(2,1)S(1)}, bf16[8,8,128]{2,1,0:T(8,128)(2,1)S(1)}, u32[]{:S(2)}, u32[]{:S(2)}) collective-permute-start(bf16[8,8,128]{2,1,0:T(8,128)(2,1)S(1)} %get-tuple-element.17), channel_id=1, source_target_pairs={{0,1},{1,2},{2,3},{3,4},{4,5},{5,6},{6,7},{8,9},{9,10},{10,11},{11... | collective-permute-start | bytes 49160 | tf_op jit(solution)/shard_map/ppermute | solution.py:18
  22.0 0.0 collective-permute-done.5
  22.0 0.6 fusion.2
  23.9 0.0 collective-permute-done.1
  23.9 0.0 copy-start.3
  23.9 0.0 collective-permute-done
  23.9 0.0 copy-start.4
  23.9 0.0 collective-permute-done.4.chi
  23.9 0.0 copy-start.5
  23.9 0.0 collective-permute-done.3.clo
  23.9 0.0 copy-start.6
  23.9 0.0 copy-done.1
  24.0 0.5 copy-done.3
  24.5 0.0 copy-done.4
  24.5 0.0 copy-done.5
  24.5 0.0 copy-done.6
  24.5 23.2 %shard_map.102 = (bf16[8,8,8,128]{3,2,1,0:T(8,128)(2,1)}, bf16[16,8,2,16,128]{4,3,2,1,0:T(8,128)(2,1)}, f32[4608,128]{1,0:T(8,128)}) custom-call(s32[26]{0:T(128)} %bitcast.42, bf16[16,8,2,16,128]{4,3,2,1,0:T(8,128)(2,1)} %bitcast.36, bf16[8,2,16,128]{3,2,1,0:T(8,128)(2,1)} %bitcast.40, bf16[8,2,16,128]{3,2,1,0:T(8,128)(2,1)} %bitcast.39, ...), custom_call_target="tpu_custom_call" | custom-call | tf_op jit(solution)/shard_map/pallas_call | solution.py:232
  47.7 1.7 %collective-permute-start.6 = (bf16[8,8,8,128]{3,2,1,0:T(8,128)(2,1)}, bf16[8,8,8,128]{3,2,1,0:T(8,128)(2,1)S(1)}, u32[]{:S(2)}, u32[]{:S(2)}) collective-permute-start(bf16[8,8,8,128]{3,2,1,0:T(8,128)(2,1)} %get-tuple-element.9), channel_id=1, source_target_pairs={{0,1},{1,0},{2,3},{3,2},{4,5},{5,4},{6,7},{7,6},{8,9},{9,8},{10,11... | collective-permute-start | bytes 393224 | tf_op jit(solution)/shard_map/ppermute | solution.py:23
  49.5 0.1 fusion.1
  49.5 0.1 broadcast_in_dim.43
  49.7 0.1 broadcast_in_dim.44
  49.8 0.1 broadcast_in_dim.49
  50.0 0.1 broadcast_in_dim.50
  50.1 0.0 copy-start
  50.1 1.7 %copy-done = f32[4608,128]{1,0:T(8,128)S(1)} copy-done((f32[4608,128]{1,0:T(8,128)S(1)}, f32[4608,128]{1,0:T(8,128)}, u32[]{:S(2)}) %copy-start) | copy-done | bytes 2359320
  51.8 0.0 copy-start.2
  51.8 32.3 %shard_map.103 = (f32[3456,128]{1,0:T(8,128)S(1)}, f32[1024,128]{1,0:T(8,128)S(1)}) custom-call(f32[4608,128]{1,0:T(8,128)S(1)} %copy-done), custom_call_target="tpu_custom_call" | custom-call | tf_op jit(solution)/shard_map/pallas_call | solution.py:344
  84.1 0.0 collective-permute-done.6
  84.1 0.2 broadcast_in_dim.52
  84.3 0.0 copy-done.2
  84.3 0.2 broadcast_in_dim.46
  84.5 2.5 %add_convert_fusion = bf16[1,1,16,16,16,128]{5,4,3,2,1,0:T(8,128)(2,1)} fusion(f32[1,1,16,16,16,128]{5,4,3,2,1,0:T(8,128)S(1)} %bitcast.34, f32[1,1,16,16,16,128]{5,4,3,2,1,0:T(8,128)S(1)} %bitcast.35, pred[16,16,16]{2,1,0:T(8,128)(4,1)S(1)} %broadcast_in_dim.50, pred[16,16,16]{2,1,0:T(8,128)(4,1)S(1)} %broadcast_in_dim.44), kind=kLoop, calls=%fused_computation | loop fusion | flops 2097152 | bytes 5251072 | tf_op jit(solution)/shard_map/convert_element_type | solution.py:411
  87.0 1.2 %copy.14 = f32[3,3,3,128,128]{4,3,2,1,0:T(8,128)} copy(f32[3,3,3,128,128]{4,3,2,1,0:T(8,128)S(1)} %bitcast.32) | data formatting | bytes 3538944
  88.2 0.8 copy.15
  (2 shorter events, 0.0 us)
Async XLA Ops:
  0.6 13.8 %collective-permute-start.2 = (bf16[16,16,16,128]{3,2,1,0:T(8,128)(2,1)}, bf16[16,16,16,128]{3,2,1,0:T(8,128)(2,1)S(1)}, u32[]{:S(2)}, u32[]{:S(2)}) collective-permute-start(bf16[16,16,16,128]{3,2,1,0:T(8,128)(2,1)} %bitcast.41), channel_id=1, source_target_pairs={{0,1},{1,0},{2,3},{3,2},{4,5},{5,4},{6,7},{7,6},{8,9},{9,8},{10,11... | collective-permute-start | bytes 3145736 | tf_op jit(solution)/shard_map/ppermute | solution.py:23
  9.1 12.9 %collective-permute-start.5 = (s32[2]{0:T(128)S(1)}, s32[2]{0:T(128)S(1)}, u32[]{:S(2)}, u32[]{:S(2)}) collective-permute-start(s32[2]{0:T(128)S(1)} %pad_add_fusion), channel_id=1, source_target_pairs={{0,1},{1,0},{2,3},{3,2},{4,5},{5,4},{6,7},{7,6},{8,9},{9,8},{10,11... | collective-permute-start | bytes 32 | tf_op jit(solution)/shard_map/ppermute | solution.py:23
  10.0 13.8 %collective-permute-start.1 = (bf16[16,16,128]{2,1,0:T(8,128)(2,1)S(1)}, bf16[16,16,128]{2,1,0:T(8,128)(2,1)S(1)}, u32[]{:S(2)}, u32[]{:S(2)}) collective-permute-start(bf16[16,16,128]{2,1,0:T(8,128)(2,1)S(1)} %get-tuple-element.14), channel_id=1, source_target_pairs={{1,0},{2,1},{3,2},{4,3},{5,4},{6,5},{7,6},{9,8},{10,9},{11,10},{12... | collective-permute-start | bytes 196616 | tf_op jit(solution)/shard_map/ppermute | solution.py:18
  11.3 12.6 %collective-permute-start = (bf16[16,16,128]{2,1,0:T(8,128)(2,1)S(1)}, bf16[16,16,128]{2,1,0:T(8,128)(2,1)S(1)}, u32[]{:S(2)}, u32[]{:S(2)}) collective-permute-start(bf16[16,16,128]{2,1,0:T(8,128)(2,1)S(1)} %get-tuple-element.15), channel_id=1, source_target_pairs={{0,1},{1,2},{2,3},{3,4},{4,5},{5,6},{6,7},{8,9},{9,10},{10,11},{11... | collective-permute-start | bytes 196616 | tf_op jit(solution)/shard_map/ppermute | solution.py:18
  15.4 8.5 %copy-start.1 = (bf16[8,8,8,128]{3,2,1,0:T(8,128)(2,1)}, bf16[8,8,8,128]{3,2,1,0:T(8,128)(2,1)S(1)}, u32[]{:S(2)}) copy-start(bf16[8,8,8,128]{3,2,1,0:T(8,128)(2,1)S(1)} %bitcast_select_fusion.ch) | copy-start | bytes 393220
  15.5 8.5 %collective-permute-start.4 = (bf16[8,8,128]{2,1,0:T(8,128)(2,1)S(1)}, bf16[8,8,128]{2,1,0:T(8,128)(2,1)S(1)}, u32[]{:S(2)}, u32[]{:S(2)}) collective-permute-start(bf16[8,8,128]{2,1,0:T(8,128)(2,1)S(1)} %get-tuple-element.16), channel_id=1, source_target_pairs={{1,0},{2,1},{3,2},{4,3},{5,4},{6,5},{7,6},{9,8},{10,9},{11,10},{12... | collective-permute-start | bytes 49160 | tf_op jit(solution)/shard_map/ppermute | solution.py:18
  16.8 7.2 %collective-permute-start.3 = (bf16[8,8,128]{2,1,0:T(8,128)(2,1)S(1)}, bf16[8,8,128]{2,1,0:T(8,128)(2,1)S(1)}, u32[]{:S(2)}, u32[]{:S(2)}) collective-permute-start(bf16[8,8,128]{2,1,0:T(8,128)(2,1)S(1)} %get-tuple-element.17), channel_id=1, source_target_pairs={{0,1},{1,2},{2,3},{3,4},{4,5},{5,6},{6,7},{8,9},{9,10},{10,11},{11... | collective-permute-start | bytes 49160 | tf_op jit(solution)/shard_map/ppermute | solution.py:18
  23.9 0.6 copy-start.3
  23.9 0.6 copy-start.4
  23.9 0.6 copy-start.5
  23.9 0.6 copy-start.6
  47.7 36.4 %collective-permute-start.6 = (bf16[8,8,8,128]{3,2,1,0:T(8,128)(2,1)}, bf16[8,8,8,128]{3,2,1,0:T(8,128)(2,1)S(1)}, u32[]{:S(2)}, u32[]{:S(2)}) collective-permute-start(bf16[8,8,8,128]{3,2,1,0:T(8,128)(2,1)} %get-tuple-element.9), channel_id=1, source_target_pairs={{0,1},{1,0},{2,3},{3,2},{4,5},{5,4},{6,7},{7,6},{8,9},{9,8},{10,11... | collective-permute-start | bytes 393224 | tf_op jit(solution)/shard_map/ppermute | solution.py:23
  50.1 1.7 %copy-start = (f32[4608,128]{1,0:T(8,128)S(1)}, f32[4608,128]{1,0:T(8,128)}, u32[]{:S(2)}) copy-start(f32[4608,128]{1,0:T(8,128)} %get-tuple-element.11.acc) | copy-start | bytes 7077892
  51.8 32.5 %copy-start.2 = (bf16[8,8,8,128]{3,2,1,0:T(8,128)(2,1)S(1)}, bf16[8,8,8,128]{3,2,1,0:T(8,128)(2,1)}, u32[]{:S(2)}) copy-start(bf16[8,8,8,128]{3,2,1,0:T(8,128)(2,1)} %get-tuple-element.9) | copy-start | bytes 393220
where the time goes:
time: 89.4 us; the launch traced here: 89 us
  Pallas kernels  55.5 us (62%)
  starting transfers between devices  13.1 us (15%)
  between operations  8.74 us (10%)
  local copies, waits for them, and re-layouts  8.01 us (9%)
  other arithmetic  3.57 us (4%)
    pallas_call x1, Pallas kernels, reduce_all(): pl.pallas_call(functools.partial(reduce_kernel, dps, zs), out_shape=(jax....  32.3 us
    pallas_call x1, Pallas kernels, compute(): pl.pallas_call(compute_kernel, out_shape=(jax.ShapeDtypeStruct((half, hal...  23.2 us
    ppermute x4, starting transfers between devices, passed_along(): return lax.ppermute(value, axis, pairs)  10.8 us
    unnamed x16, local copies, waits for them, and re-layouts  4.26 us
    convert_element_type x1, other arithmetic, local(): coarse.astype(BF16).reshape(1, 1, edge, edge, edge, c)  2.46 us
    ppermute x3, starting transfers between devices, partner(): return lax.ppermute(block, axis, [(i, i ^ 1) for i in range(count)])  2.32 us
  transfers between devices with their start and end apart: 7, of which 0 were waited for; matrix products, arithmetic and copies ran while one was open for 5% of the time, Pallas kernels for 36%

commit v1 on v0

v1 whole, which is shorter than its diff:
```python
import functools

import jax
import jax.numpy as jnp
from jax import lax
from jax.experimental import pallas as pl
from jax.experimental.pallas import tpu as pltpu
from jax.sharding import PartitionSpec as P

loss_scale = 1024.0
MESH = pl.DeviceIdType.MESH
F32, BF16 = jnp.float32, jnp.bfloat16


def nn(a, b):
    return lax.dot_general(a, b, (((1,), (0,)), ((), ())), preferred_element_type=F32)


def nt(a, b):
    return lax.dot_general(a, b, (((1,), (1,)), ((), ())), preferred_element_type=F32)


def shifted(s, low, mid, high):
    edge = s.shape[-2]
    axis = s.ndim - 2
    row = lax.broadcasted_iota(jnp.int32, s.shape, axis)
    first = pltpu.roll(s, 1, axis) * jnp.where(row == 0, low, mid)
    last = pltpu.roll(s, edge - 1, axis) * jnp.where(row == edge - 1, high, mid)
    return first, s * mid, last


def put_plane(dst, x, even, odd, low, mid, high):
    half, c = even.shape[0], even.shape[-1]
    for k, v in enumerate(shifted(even, low, mid, high)):
        dst[x, 0:half, :, 2 * k * c + c : 2 * k * c + 2 * c] = v.astype(BF16)
    for k, v in enumerate(shifted(odd, low, mid, high)):
        dst[x, 1 : half + 1, :, 2 * k * c : 2 * k * c + c] = v.astype(BF16)


def put_row(dst, x, y, row, low, mid, high):
    c = row.shape[-1]
    for k, v in enumerate(shifted(row, low, mid, high)):
        at = 2 * k * c + (y % 2) * c
        dst[x, y // 2, :, at : at + c] = v.astype(BF16)


def masks(nb, a):
    def m(b, c):
        i = (a + 1) * 9 + (b + 1) * 3 + (c + 1)
        i = i - 1 if i > 13 else i
        return jnp.where(nb[i] >= 0, 1.0, 0.0).astype(F32)

    return {b: (m(b, -1), m(b, 0), m(b, 1)) for b in (-1, 0, 1)}


def put_halo(dst, x, even, odd, mask):
    half, edge = even.shape[0], dst.shape[0]
    put_plane(dst, x, even, odd, *mask[0])
    put_row(dst, x, 0, odd[half - 1], *mask[-1])
    put_row(dst, x, edge - 1, even[0], *mask[1])


def zero_rows(dst, edge, c):
    z = jnp.zeros((edge, dst.shape[2], c), BF16)
    for k in range(3):
        dst[1 : edge + 1, 0, :, 2 * k * c : 2 * k * c + c] = z
        dst[1 : edge + 1, edge // 2, :, 2 * k * c + c : 2 * k * c + 2 * c] = z


def tap_of(s, pin, pout):
    b = 2 * s + pin - pout
    return b if 0 <= b <= 2 else None


class Reduction:
    def __init__(self, env, acc, whole, start, n, refs):
        self.env, self.acc, self.whole, self.start = env, acc, whole, start
        (self.to_core, self.from_core, self.to_dp, self.from_dp, self.to_z, self.from_z) = refs[:6]
        self.sems = refs[6:]
        self.h = n // 2
        self.q = self.h // env.dps
        self.s = self.q // env.zs
        self.half = self.start + env.core * self.h
        self.quarter = self.half + env.dp * self.q
        self.piece = self.quarter + env.z * self.s
        self.flying = []

    def go(self, stage, src, dst, peers):
        send, recv = self.sems[2 * stage], self.sems[2 * stage + 1]
        self.flying = [
            self.env.send(src(k), dst(k), send.at[k - 1], recv.at[k - 1], to)
            for k, to in enumerate(peers, 1)
        ]

    def land(self):
        for copy in self.flying:
            copy.wait()

    def spread(self, stage, at, n, peers):
        ref = self.whole.at[rows_at(at, n)]
        self.go(stage, lambda k: ref, lambda k: ref, peers)

    def step(self, stage):
        env, acc = self.env, self.acc
        h, q, s = self.h, self.q, self.s
        if stage > 0:
            self.land()
        if stage == 0:
            self.to_core[...] = acc[rows_at(self.start + (1 - env.core) * h, h)].astype(BF16)
            self.go(0, lambda k: self.to_core, lambda k: self.from_core, [env.mate])
        elif stage == 1:
            part = acc[rows_at(self.half, h)] + self.from_core[...].astype(F32)
            acc[rows_at(self.half, h)] = part
            self.to_dp[...] = part.astype(BF16)
            self.go(
                1,
                lambda k: self.to_dp.at[rows_at(env.dp_at(k) * q, q)],
                lambda k: self.from_dp.at[k - 1],
                env.dp_peers,
            )
        elif stage == 2:
            part = acc[rows_at(self.quarter, q)]
            for k in range(1, env.dps):
                part += self.from_dp[k - 1].astype(F32)
            acc[rows_at(self.quarter, q)] = part
            self.to_z[...] = part.astype(BF16)
            self.go(
                2,
                lambda k: self.to_z.at[rows_at(env.z_at(k) * s, s)],
                lambda k: self.from_z.at[k - 1],
                env.z_peers,
            )
        elif stage == 3:
            part = acc[rows_at(self.piece, s)]
            for k in range(1, env.zs):
                part += self.from_z[k - 1].astype(F32)
            self.whole[rows_at(self.piece, s)] = part.astype(BF16)
            self.spread(3, self.piece, s, env.z_peers)
        elif stage == 4:
            self.spread(4, self.quarter, q, env.dp_peers)
        elif stage == 5:
            self.spread(5, self.half, h, [env.mate])


def reduction_scratch(n, dps, zs, c):
    h = n // 2
    q = h // dps
    s = q // zs
    out = [
        pltpu.VMEM((h, c), BF16),
        pltpu.VMEM((h, c), BF16),
        pltpu.VMEM((h, c), BF16),
        pltpu.VMEM((dps - 1, q, c), BF16),
        pltpu.VMEM((q, c), BF16),
        pltpu.VMEM((zs - 1, s, c), BF16),
    ]
    for k in (1, dps - 1, zs - 1, zs - 1, dps - 1, 1):
        out += [pltpu.SemaphoreType.DMA((k,))] * 2
    return out


REDUCTION_REFS = 18


def rows_at(start, n):
    return pl.ds(pl.multiple_of(start, 16) if not isinstance(start, int) else start, n)


class Peers:
    def __init__(self, dps, zs):
        self.dps, self.zs = dps, zs
        n = 2 * zs
        self.dp, self.region = lax.axis_index("dp"), lax.axis_index("region")
        self.core, self.z = lax.rem(self.region, 2), lax.div(self.region, 2)
        self.mate = (self.dp, self.region + 1 - 2 * self.core)
        self.right = (self.dp, lax.rem(self.region + 1, n))
        self.left = (self.dp, lax.rem(self.region + n - 1, n))
        self.dp_peers = [(self.dp_at(k), self.region) for k in range(1, dps)]
        self.z_peers = [(self.dp, 2 * self.z_at(k) + self.core) for k in range(1, zs)]

    def dp_at(self, k):
        return lax.rem(self.dp + k, self.dps)

    def z_at(self, k):
        return lax.rem(self.z + k, self.zs)

    def enter(self):
        barrier = pltpu.get_barrier_semaphore()
        peers = [self.mate, self.right, self.left] + self.dp_peers + self.z_peers
        for peer in peers:
            pl.semaphore_signal(barrier, inc=1, device_id=peer, device_id_type=MESH)
        pl.semaphore_wait(barrier, len(peers))

    def send(self, src, dst, send, recv, to):
        copy = pltpu.make_async_remote_copy(
            src_ref=src, dst_ref=dst, send_sem=send, recv_sem=recv,
            device_id=to, device_id_type=MESH,
        )
        copy.start()
        return copy


def kernel(
    sizes, nb, own, f, cot, tag, cw, dw,
    coarse, ig, conv, down,
    field, wide, gfold, up, outf, gt, tt, acc, whole,
    flo, fhi, cot2, tag2, ch, clo, chi, blocks, blocks2, sends, recvs, *refs
):
    dps, zs, cut, conv_rows, down_rows = sizes
    env = Peers(dps, zs)
    edge, c = f.shape[0], f.shape[-1]
    half = edge // 2
    rows = half * edge
    n = REDUCTION_REFS
    first = Reduction(env, acc, whole, 0, cut, refs[:n])
    second = Reduction(env, acc, whole, cut, conv_rows - cut, refs[n : 2 * n])
    third = Reduction(env, acc, whole, conv_rows, down_rows, refs[2 * n :])

    def send(i, src, dst, to):
        return env.send(src, dst, sends.at[i], recvs.at[i], to)

    env.enter()
    cot_copy = send(0, cot, cot2, env.mate)
    tag_copy = send(1, tag, tag2, env.mate)
    up_copy = send(2, f.at[edge - 1], flo, env.right)
    down_copy = send(3, f.at[0], fhi, env.left)

    def window(x, m, a, s):
        return field[pl.ds(x + a, m), s : s + half].reshape(m * rows, 6 * c)

    def lhs(x, m):
        return jnp.concatenate([window(x, m, a, s) for a in range(3) for s in range(2)], -1)

    below, above = masks(nb, -1), masks(nb, 1)
    zero_rows(field, edge, c)

    @pl.loop(0, edge)
    def _(x):
        put_plane(field, x + 1, f[x, :, 0].astype(F32), f[x, :, 1].astype(F32), 0.0, 1.0, 0.0)

    zero = jnp.zeros((c, c), BF16)

    def weights(block):
        for a in range(3):
            for s in range(2):
                for k in range(3):
                    for pin in range(2):
                        at = ((2 * a + s) * 3 + k) * 2 * c + pin * c
                        for pout in range(2):
                            b = tap_of(s, pin, pout)
                            wide[at : at + c, pout * c : (pout + 1) * c] = (
                                zero if b is None else block(a, b, k)
                            )

    weights(lambda a, b, k: cw[9 * a + 3 * b + k])

    cot_copy.wait()
    tag_copy.wait()
    octant, home = own[1], own[0] == env.region
    picked = jnp.zeros((half, half, half, c), F32)
    for o in range(4):
        cut_of = (slice((o // 2) * half, (o // 2 + 1) * half), slice(o % 2 * half, (o % 2 + 1) * half))
        mine, theirs = cot[cut_of].astype(F32), cot2[cut_of].astype(F32)
        both = jnp.where(home, mine, theirs)
        for z in range(2):
            picked = jnp.where(
                octant == 2 * o + z, both[:, :, z * half : (z + 1) * half], picked
            )
    ch[...] = picked.astype(BF16)
    clo_copy = send(4, ch.at[half - 1], clo, env.right)
    chi_copy = send(5, ch.at[0], chi, env.left)

    up[...] = jnp.zeros_like(up)

    def lift(v):
        m = v.shape[0] * v.shape[1]
        v = v.astype(F32).reshape(m, half, c)
        for r in range(2):
            up[r, 0:m, pl.ds(r, half, 2), :] = v
        both = [up[r, 0:m].reshape(m * edge, c).astype(BF16) for r in range(2)]
        return jnp.concatenate(both, -1)

    def dwt(p):
        return jnp.concatenate(
            [jnp.concatenate([dw[4 * p + 2 * q + r] for r in range(2)], -1) for q in range(2)], 0
        )

    raised = lift(picked)
    for p in range(2):
        g = nt(raised, dwt(p)).astype(BF16).reshape(half, half, edge, 2 * c)
        for i in range(half):
            gfold[2 * i + p] = g[i]

    up_copy.wait()
    down_copy.wait()
    put_halo(field, 0, flo[:, 0].astype(F32), flo[:, 1].astype(F32), below)
    put_halo(field, edge + 1, fhi[:, 0].astype(F32), fhi[:, 1].astype(F32), above)

    flat = gfold[...].reshape(edge * rows, 2 * c)
    gt[...] = flat.astype(F32).T.astype(BF16)
    for a in range(3):
        for s in range(2):
            tt[s] = nn(gt[...], window(0, edge, a, s))
        for b in range(3):
            for k in range(3):
                total = jnp.zeros((c, c), F32)
                for s in range(2):
                    for pin in range(2):
                        for pout in range(2):
                            if tap_of(s, pin, pout) == b:
                                at = (2 * k + pin) * c
                                total += tt[s, pout * c : (pout + 1) * c, at : at + c]
                tap = 9 * a + 3 * b + k
                acc[tap * c : (tap + 1) * c] = total.T * (1.0 / loss_scale)
        if a == 1:
            first.step(0)
    if conv_rows > 27 * c:
        acc[27 * c : conv_rows] = jnp.zeros((conv_rows - 27 * c, c), F32)
    second.step(0)
    first.step(1)

    step = 4

    def forward(m, to):
        @pl.loop(m, to)
        def _(i):
            x = i * step
            out = nn(lhs(x, step), wide[...]).reshape(step, half, edge, 2 * c)
            for q in range(2):
                outf[q, pl.ds(x, step)] = (
                    (out[..., q * c : (q + 1) * c] + f[pl.ds(x, step), :, q].astype(F32))
                    .astype(BF16)
                    .astype(F32)
                )

    laps = edge // step
    forward(0, laps // 2)
    second.step(1)
    forward(laps // 2, laps)
    first.step(2)

    taken = []
    for p in range(2):
        for r in range(2):
            halves = []
            for q in range(2):
                parts = [
                    outf[q, 2 * i + p, :, pl.ds(r, half, 2), :].reshape(half * half, c)
                    for i in range(half)
                ]
                halves.append(jnp.concatenate(parts, 0).astype(BF16))
            taken.append(jnp.concatenate(halves, -1))
    dwf = jnp.concatenate(
        [dw[4 * p + 2 * q + r] for p in range(2) for r in range(2) for q in range(2)], 0
    )
    blocks[...] = nn(jnp.concatenate(taken, -1), dwf).astype(BF16).reshape(blocks.shape)
    blocks_copy = send(6, blocks, blocks2, env.mate)
    cht = ch[...].reshape(half**3, c).astype(F32).T.astype(BF16)
    for p in range(2):
        for r in range(2):
            d = nn(cht, taken[2 * p + r])
            for q in range(2):
                at = conv_rows + (4 * p + 2 * q + r) * c
                acc[at : at + c] = d[:, q * c : (q + 1) * c].T * (1.0 / loss_scale)
    if down_rows > 8 * c:
        acc[conv_rows + 8 * c :] = jnp.zeros((down_rows - 8 * c, c), F32)
    third.step(0)
    second.step(2)

    clo_copy.wait()
    chi_copy.wait()
    for edge_of, p, x, mask in ((clo, 1, 0, below), (chi, 0, edge + 1, above)):
        g = nt(lift(edge_of[...][None]), dwt(p)).astype(BF16).astype(F32)
        g = g.reshape(half, edge, 2 * c)
        put_halo(field, x, g[..., :c], g[..., c:], mask)

    @pl.loop(0, edge)
    def _(x):
        g = gfold[x].astype(F32)
        put_plane(field, x + 1, g[..., :c], g[..., c:], 0.0, 1.0, 0.0)

    third.step(1)
    first.step(3)
    weights(lambda a, b, k: cw[9 * (2 - a) + 3 * (2 - b) + 2 - k].T)
    second.step(3)

    def backward(m, to):
        @pl.loop(m, to)
        def _(i):
            x = i * step
            out = nn(lhs(x, step), wide[...]).reshape(step, half, edge, 2 * c)
            out = (out + gfold[pl.ds(x, step)].astype(F32)).astype(BF16)
            for q in range(2):
                ig[pl.ds(x, step), :, q] = out[..., q * c : (q + 1) * c]

    backward(0, laps // 2)
    first.step(4)
    third.step(2)
    second.step(4)
    backward(laps // 2, laps)
    third.step(3)
    first.step(5)

    blocks_copy.wait()
    mine, theirs = blocks[...].astype(F32), blocks2[...].astype(F32)
    own_tag, other_tag = tag[0:1, :], tag2[0:1, :]
    third.step(4)
    second.step(5)
    for o in range(4):
        parts = []
        for z in range(2):
            here = env.region * 8 + 2 * o + z
            ours = jnp.where(own_tag == here, 1.0, 0.0).astype(F32)
            others = jnp.where(other_tag == here, 1.0, 0.0).astype(F32)
            parts.append(mine * ours + theirs * others)
        x, y = o // 2 * half, o % 2 * half
        coarse[x : x + half, y : y + half] = jnp.concatenate(parts, 2).astype(BF16)
    third.step(5)
    first.land()
    conv[:cut] = whole[:cut].astype(F32)
    second.land()
    conv[cut:] = whole[cut : conv.shape[0]].astype(F32)
    third.land()
    down[...] = whole[conv_rows : conv_rows + down.shape[0]].astype(F32)


def local(features, conv_weight, down_weight, coarse_cotangent, brick_coords, neighbours, parents):
    edge, c = features.shape[2], features.shape[-1]
    half = edge // 2
    dps, regions = lax.axis_size("dp"), lax.axis_size("region")
    zs = regions // 2
    unit = 16 * dps * regions
    cut = 18 * c // unit * unit
    conv_rows = -(-27 * c // unit) * unit
    down_rows = -(-8 * c // unit) * unit
    xyz = brick_coords.reshape(3)
    octant = xyz[0] % 2 * 4 + xyz[1] % 2 * 2 + xyz[2] % 2
    parent = parents.reshape(())
    own = jnp.stack([parent, octant])
    tag = jnp.broadcast_to(parent * 8 + octant, (8, 128)).astype(jnp.int32)
    vmem = pl.BlockSpec(memory_space=pltpu.VMEM)
    smem = pl.BlockSpec(memory_space=pltpu.SMEM)
    plane = pltpu.VMEM((half, 2, edge, c), BF16)
    cube = pltpu.VMEM((half, half, half, c), BF16)
    layer = pltpu.VMEM((half, half, c), BF16)
    scratch = [
        pltpu.VMEM((edge + 2, half + 1, edge, 6 * c), BF16),
        pltpu.VMEM((36 * c, 2 * c), BF16),
        pltpu.VMEM((edge, half, edge, 2 * c), BF16),
        pltpu.VMEM((2, half * half, edge, c), F32),
        pltpu.VMEM((2, edge, half, edge, c), F32),
        pltpu.VMEM((2 * c, edge * half * edge), BF16),
        pltpu.VMEM((2, 2 * c, 6 * c), F32),
        pltpu.VMEM((conv_rows + down_rows, c), F32),
        pltpu.VMEM((conv_rows + down_rows, c), BF16),
        plane,
        plane,
        pltpu.VMEM((edge, edge, edge, c), BF16),
        pltpu.VMEM((8, 128), jnp.int32),
        cube,
        layer,
        layer,
        cube,
        cube,
        pltpu.SemaphoreType.DMA((7,)),
        pltpu.SemaphoreType.DMA((7,)),
    ]
    for n in (cut, conv_rows - cut, down_rows):
        scratch += reduction_scratch(n, dps, zs, c)
    coarse, ig, conv_total, down_total = pl.pallas_call(
        functools.partial(kernel, (dps, zs, cut, conv_rows, down_rows)),
        out_shape=(
            jax.ShapeDtypeStruct((edge, edge, edge, c), BF16),
            jax.ShapeDtypeStruct((edge, half, 2, edge, c), BF16),
            jax.ShapeDtypeStruct((27 * c, c), F32),
            jax.ShapeDtypeStruct((8 * c, c), F32),
        ),
        in_specs=[smem, smem] + [vmem] * 5,
        out_specs=(vmem,) * 4,
        scratch_shapes=scratch,
        compiler_params=pltpu.CompilerParams(
            collective_id=0, has_side_effects=True, vmem_limit_bytes=60 * 1024 * 1024
        ),
    )(
        neighbours.reshape(26), own, features.reshape(edge, half, 2, edge, c),
        coarse_cotangent.reshape(edge, edge, edge, c), tag,
        conv_weight.reshape(27, c, c), down_weight.reshape(8, c, c),
    )
    return (
        coarse.reshape(1, 1, edge, edge, edge, c),
        ig.reshape(1, 1, edge, edge, edge, c),
        conv_total.reshape(3, 3, 3, c, c),
        down_total.reshape(2, 2, 2, c, c),
    )


def solution(mesh):
    in_specs = (
        P("dp", "region", None, None, None, None),
        P(),
        P(),
        P("dp", "region", None, None, None, None),
        P("dp", "region", None),
        P("dp", "region", None),
        P("dp", "region"),
    )
    out_specs = (
        P("dp", "region", None, None, None, None),
        P("dp", "region", None, None, None, None),
        P(),
        P(),
    )
    return jax.shard_map(local, mesh=mesh, in_specs=in_specs, out_specs=out_specs, check_vma=False)
```

time: 89.4 us -> 61 us (0.68)
  starting transfers between devices: 13.1 us -> 0 us
  Pallas kernels: 55.5 us -> 45.2 us
  other arithmetic: 3.57 us -> 0.59 us
  between operations: 8.74 us -> 7.17 us
    ppermute x7 -> x0, starting transfers between devices: 13.1 us -> none  [the longest x4 10.8 us: passed_along(): return lax.ppermute(value, axis, pairs)]
    pallas_call x2 -> x1, Pallas kernels: 55.5 us -> 45.2 us  [local(): pl.pallas_call(functools.partial(kernel, (dps, zs, cut, conv_rows, down_r...]
    convert_element_type x1 -> x0, other arithmetic: 2.46 us -> none  [local(): coarse.astype(BF16).reshape(1, 1, edge, edge, edge, c)]
    unnamed x16 -> x10, local copies, waits for them, and re-layouts: 4.26 us -> 5.74 us
    select_n x1 -> x0, other arithmetic: 0.96 us -> none  [local(): jnp.where(at_home, octants(cot, octant), octants(other_cot, octant))]
  transfers between devices with their start and end apart: 7 -> 0, of which waited for: 0 -> 0; matrix products, arithmetic and copies ran while one was open for 5% -> 0% of each run, Pallas kernels for 36% -> 0%
where the time goes in v1:
time: 61 us; the launch traced here: 60.7 us
  Pallas kernels  45.2 us (74%)
  local copies, waits for them, and re-layouts  7.69 us (13%)
  between operations  7.17 us (12%)
    pallas_call x1, Pallas kernels, local(): pl.pallas_call(functools.partial(kernel, (dps, zs, cut, conv_rows, down_r...  45.2 us
    unnamed x10, local copies, waits for them, and re-layouts  5.74 us
    slice x1, local copies, waits for them, and re-layouts, local(): octant = xyz[0] % 2 * 4 + xyz[1] % 2 * 2 + xyz[2] % 2  1.35 us

profile of v1, /device:TPU:0, one launch (start us, length us, event | category | flops | bytes accessed | tf_op | source)
XLA Modules:
  0.0 60.7 jit_solution(1145342643804772356)
XLA Ops:
  1.3 1.4 %fusion = (s32[1,1,1]{2,1,0:T(1,128)}, s32[1,1,1]{2,1,0:T(1,128)}, s32[1,1,1]{2,1,0:T(1,128)}) fusion(s32[1,1,3]{2,1,0:T(1,128)} %param.11), kind=kLoop, calls=%fused_computation.1 | loop fusion | bytes 24 | tf_op jit(solution)/shard_map/slice | solution.py:437
  8.5 0.6 pad_add_fusion.own
  9.1 0.6 broadcast_in_dim.3.tag
  9.7 45.2 %shard_map.102 = (bf16[16,16,16,128]{3,2,1,0:T(8,128)(2,1)}, bf16[16,8,2,16,128]{4,3,2,1,0:T(8,128)(2,1)}, f32[3456,128]{1,0:T(8,128)}, f32[1024,128]{1,0:T(8,128)}) custom-call(s32[26]{0:T(128)} %bitcast.24, s32[2]{0:T(128)} %pad_add_fusion.own, bf16[16,8,2,16,128]{4,3,2,1,0:T(8,128)(2,1)} %bitcast.17, bf16[16,16,16,128]{3,2,1,0:T(8,128)(2,1)} %bitcast.18, ...), custom_call_target="tpu_custom_call" | custom-call | tf_op jit(solution)/shard_map/pallas_call | solution.py:470
  54.9 0.0 copy-start.1
  54.9 0.0 copy-start
  54.9 2.6 %copy.16 = bf16[1,1,16,16,16,128]{5,4,3,2,1,0:T(8,128)(2,1)} copy(bf16[1,1,16,16,16,128]{5,4,3,2,1,0:T(8,128)(2,1)} %bitcast.20) | data formatting | bytes 2097152
  57.5 0.0 copy-done.1
  57.5 1.0 %copy.17 = bf16[1,1,16,16,16,128]{5,4,3,2,1,0:T(8,128)(2,1)} copy(bf16[1,1,16,16,16,128]{5,4,3,2,1,0:T(8,128)(2,1)S(1)} %bitcast.19) | data formatting | bytes 2097152
  58.5 0.0 copy-done
  58.5 0.0 copy-start.2
  58.5 1.2 %copy.18 = f32[3,3,3,128,128]{4,3,2,1,0:T(8,128)} copy(f32[3,3,3,128,128]{4,3,2,1,0:T(8,128)S(1)} %bitcast.16) | data formatting | bytes 3538944
  59.7 0.2 copy-done.2
  59.9 0.8 %copy.19 = f32[2,2,2,128,128]{4,3,2,1,0:T(8,128)} copy(f32[2,2,2,128,128]{4,3,2,1,0:T(8,128)S(1)} %bitcast.22) | data formatting | bytes 1048576
Async XLA Ops:
  54.9 2.6 %copy-start.1 = (bf16[16,8,2,16,128]{4,3,2,1,0:T(8,128)(2,1)S(1)}, bf16[16,8,2,16,128]{4,3,2,1,0:T(8,128)(2,1)}, u32[]{:S(2)}) copy-start(bf16[16,8,2,16,128]{4,3,2,1,0:T(8,128)(2,1)} %get-tuple-element.9) | copy-start | bytes 3145732
  54.9 3.6 %copy-start = (f32[3456,128]{1,0:T(8,128)S(1)}, f32[3456,128]{1,0:T(8,128)}, u32[]{:S(2)}) copy-start(f32[3456,128]{1,0:T(8,128)} %get-tuple-element.10) | copy-start | bytes 5308420
  58.5 1.4 %copy-start.2 = (f32[1024,128]{1,0:T(8,128)S(1)}, f32[1024,128]{1,0:T(8,128)}, u32[]{:S(2)}) copy-start(f32[1024,128]{1,0:T(8,128)} %get-tuple-element.11) | copy-start | bytes 1572868

commit v2 on v1

--- a/solution.py
+++ b/solution.py
@@ -201,10 +201,10 @@
 
 
 def kernel(
-    sizes, nb, own, f, cot, tag, cw, dw,
+    sizes, nb, xyz, parent, f, cot, cw, dw,
     coarse, ig, conv, down,
     field, wide, gfold, up, outf, gt, tt, acc, whole,
-    flo, fhi, cot2, tag2, ch, clo, chi, blocks, blocks2, sends, recvs, *refs
+    flo, fhi, cot2, tag, tag2, ch, clo, chi, blocks, blocks2, sends, recvs, *refs
 ):
     dps, zs, cut, conv_rows, down_rows = sizes
     env = Peers(dps, zs)
@@ -219,6 +219,8 @@
     def send(i, src, dst, to):
         return env.send(src, dst, sends.at[i], recvs.at[i], to)
 
+    octant = lax.rem(xyz[0], 2) * 4 + lax.rem(xyz[1], 2) * 2 + lax.rem(xyz[2], 2)
+    tag[...] = jnp.full(tag.shape, parent[0] * 8 + octant, jnp.int32)
     env.enter()
     cot_copy = send(0, cot, cot2, env.mate)
     tag_copy = send(1, tag, tag2, env.mate)
@@ -256,7 +258,7 @@
 
     cot_copy.wait()
     tag_copy.wait()
-    octant, home = own[1], own[0] == env.region
+    home = parent[0] == env.region
     picked = jnp.zeros((half, half, half, c), F32)
     for o in range(4):
         cut_of = (slice((o // 2) * half, (o // 2 + 1) * half), slice(o % 2 * half, (o % 2 + 1) * half))
@@ -393,19 +395,22 @@
             for q in range(2):
                 ig[pl.ds(x, step), :, q] = out[..., q * c : (q + 1) * c]
 
-    backward(0, laps // 2)
+    quarter = laps // 4
+    backward(0, quarter)
+    third.step(2)
     first.step(4)
-    third.step(2)
+    backward(quarter, 2 * quarter)
     second.step(4)
-    backward(laps // 2, laps)
+    backward(2 * quarter, 3 * quarter)
     third.step(3)
     first.step(5)
+    backward(3 * quarter, laps)
+    third.step(4)
+    second.step(5)
 
     blocks_copy.wait()
     mine, theirs = blocks[...].astype(F32), blocks2[...].astype(F32)
     own_tag, other_tag = tag[0:1, :], tag2[0:1, :]
-    third.step(4)
-    second.step(5)
     for o in range(4):
         parts = []
         for z in range(2):
@@ -433,11 +438,6 @@
     cut = 18 * c // unit * unit
     conv_rows = -(-27 * c // unit) * unit
     down_rows = -(-8 * c // unit) * unit
-    xyz = brick_coords.reshape(3)
-    octant = xyz[0] % 2 * 4 + xyz[1] % 2 * 2 + xyz[2] % 2
-    parent = parents.reshape(())
-    own = jnp.stack([parent, octant])
-    tag = jnp.broadcast_to(parent * 8 + octant, (8, 128)).astype(jnp.int32)
     vmem = pl.BlockSpec(memory_space=pltpu.VMEM)
     smem = pl.BlockSpec(memory_space=pltpu.SMEM)
     plane = pltpu.VMEM((half, 2, edge, c), BF16)
@@ -457,6 +457,7 @@
         plane,
         pltpu.VMEM((edge, edge, edge, c), BF16),
         pltpu.VMEM((8, 128), jnp.int32),
+        pltpu.VMEM((8, 128), jnp.int32),
         cube,
         layer,
         layer,
@@ -475,15 +476,15 @@
             jax.ShapeDtypeStruct((27 * c, c), F32),
             jax.ShapeDtypeStruct((8 * c, c), F32),
         ),
-        in_specs=[smem, smem] + [vmem] * 5,
+        in_specs=[smem] * 3 + [vmem] * 4,
         out_specs=(vmem,) * 4,
         scratch_shapes=scratch,
         compiler_params=pltpu.CompilerParams(
             collective_id=0, has_side_effects=True, vmem_limit_bytes=60 * 1024 * 1024
         ),
     )(
-        neighbours.reshape(26), own, features.reshape(edge, half, 2, edge, c),
-        coarse_cotangent.reshape(edge, edge, edge, c), tag,
+        neighbours.reshape(26), brick_coords.reshape(3), parents.reshape(1),
+        features.reshape(edge, half, 2, edge, c), coarse_cotangent.reshape(edge, edge, edge, c),
         conv_weight.reshape(27, c, c), down_weight.reshape(8, c, c),
     )
     return (

time: 61 us -> 53.9 us (0.88)
  between operations: 7.17 us -> 1.31 us
  local copies, waits for them, and re-layouts: 7.69 us -> 5.74 us
  Pallas kernels: 45.2 us -> 46.6 us
    pallas_call x1, Pallas kernels: 45.2 us -> 46.6 us  [local(): pl.pallas_call(functools.partial(kernel, (dps, zs, cut, conv_rows, down_r...]
    slice x1 -> x0, local copies, waits for them, and re-layouts: 1.35 us -> none  [local(): octant = xyz[0] % 2 * 4 + xyz[1] % 2 * 2 + xyz[2] % 2]
where the time goes in v2:
time: 53.9 us; the launch traced here: 53.7 us
  Pallas kernels  46.6 us (86%)
  local copies, waits for them, and re-layouts  5.74 us (11%)
  between operations  1.31 us (2%)
    pallas_call x1, Pallas kernels, local(): pl.pallas_call(functools.partial(kernel, (dps, zs, cut, conv_rows, down_r...  46.6 us
    unnamed x10, local copies, waits for them, and re-layouts  5.74 us

profile of v2, /device:TPU:0, one launch (start us, length us, event | category | flops | bytes accessed | tf_op | source)
XLA Modules:
  0.0 53.7 jit_solution(17416912949813371278)
XLA Ops:
  1.3 46.6 %shard_map.102 = (bf16[16,16,16,128]{3,2,1,0:T(8,128)(2,1)}, bf16[16,8,2,16,128]{4,3,2,1,0:T(8,128)(2,1)}, f32[3456,128]{1,0:T(8,128)}, f32[1024,128]{1,0:T(8,128)}) custom-call(s32[26]{0:T(128)} %bitcast.20, s32[3]{0:T(128)} %bitcast.21, s32[1]{0:T(128)} %bitcast.11.parent, bf16[16,8,2,16,128]{4,3,2,1,0:T(8,128)(2,1)} %bitcast.13, ...), custom_call_target="tpu_custom_call" | custom-call | tf_op jit(solution)/shard_map/pallas_call | solution.py:471
  47.9 0.0 copy-start.1
  47.9 0.0 copy-start
  47.9 2.6 %copy.16 = bf16[1,1,16,16,16,128]{5,4,3,2,1,0:T(8,128)(2,1)} copy(bf16[1,1,16,16,16,128]{5,4,3,2,1,0:T(8,128)(2,1)} %bitcast.16) | data formatting | bytes 2097152
  50.5 0.0 copy-done.1
  50.5 1.0 %copy.17 = bf16[1,1,16,16,16,128]{5,4,3,2,1,0:T(8,128)(2,1)} copy(bf16[1,1,16,16,16,128]{5,4,3,2,1,0:T(8,128)(2,1)S(1)} %bitcast.15) | data formatting | bytes 2097152
  51.5 0.0 copy-done
  51.5 0.0 copy-start.2
  51.5 1.2 %copy.18 = f32[3,3,3,128,128]{4,3,2,1,0:T(8,128)} copy(f32[3,3,3,128,128]{4,3,2,1,0:T(8,128)S(1)} %bitcast.12) | data formatting | bytes 3538944
  52.7 0.2 copy-done.2
  52.9 0.8 %copy.19 = f32[2,2,2,128,128]{4,3,2,1,0:T(8,128)} copy(f32[2,2,2,128,128]{4,3,2,1,0:T(8,128)S(1)} %bitcast.18) | data formatting | bytes 1048576
Async XLA Ops:
  47.9 2.6 %copy-start.1 = (bf16[16,8,2,16,128]{4,3,2,1,0:T(8,128)(2,1)S(1)}, bf16[16,8,2,16,128]{4,3,2,1,0:T(8,128)(2,1)}, u32[]{:S(2)}) copy-start(bf16[16,8,2,16,128]{4,3,2,1,0:T(8,128)(2,1)} %get-tuple-element.9) | copy-start | bytes 3145732
  47.9 3.6 %copy-start = (f32[3456,128]{1,0:T(8,128)S(1)}, f32[3456,128]{1,0:T(8,128)}, u32[]{:S(2)}) copy-start(f32[3456,128]{1,0:T(8,128)} %get-tuple-element.10) | copy-start | bytes 5308420
  51.5 1.4 %copy-start.2 = (f32[1024,128]{1,0:T(8,128)S(1)}, f32[1024,128]{1,0:T(8,128)}, u32[]{:S(2)}) copy-start(f32[1024,128]{1,0:T(8,128)} %get-tuple-element.11) | copy-start | bytes 1572868
